TPU v7x, 512 devices: a whole 4x8x8 slice. The times are simulated.
512 devices in a mesh: dp: 4 (over x_hi, core), context: 16 (over x_lo, z), tensor: 8 (over y).
Axes of the slice: x: 4 (x_hi: 2, x_lo: 2; x = x_hi * 2 + x_lo), y: 8, z: 8, core: 2. Of those that a mesh axis runs over, the one named last changes fastest.
Arguments:
- tokens: bfloat16 [32768, 4096], P(('dp', 'context', 'tensor')), parts along dimension 0, may hold values from -6 to 6
- norm_gain: bfloat16 [4096], replicated, may hold values from 0.099609375 to 1.8984375
- w_query: bfloat16 [4096, 2048], P(None, 'tensor'), may hold values from -2.03125 to 2.03125
- key_matrix: bfloat16 [4096, 1024], P(None, 'tensor'), may hold values from -0.109375 to 0.109375
- value_matrix: bfloat16 [4096, 1024], P(None, 'tensor'), may hold values from -0.09375 to 0.09375
- seg_ids: int32 [32768], P('dp'), parts along dimension 0, may hold values from 0 to 7, never falling along the last dimension, each value on 1 to 4096 neighbouring positions
Outputs:
- attended: bfloat16 [32768, 2048], P(('dp', 'context'), 'tensor'), parts along dimension 0
There are 4 independent parts, one for each index of `dp`. A program takes and returns all parts, laid end to end along the dimension named above; an argument that names none is the same for every part. Nothing has to cross between parts.
Inputs may be any that keep to these rules, and one draw needn't show every extreme that they name: `seg_ids`: never falls along the row; each of the 8 documents covers 1 to 4096 positions, one exactly 4096.
All inputs are finite; a program needn't handle non-finite values.
Results may differ from a plain program's by a relative error of at most 0.0078.
Values may be sent and summed in bfloat16 or wider, within the bound.
A program may use at most 64 MiB of HBM per device.

v0:
```python
import math

import jax
import jax.numpy as jnp
from jax import lax
from jax.sharding import PartitionSpec as P

HEAD_SIZE = 128


def sent_together(arrays, axis, dim, along):
    widths = [a.shape[along] for a in arrays]
    both = jnp.concatenate(arrays, axis=along)
    filled = lax.all_gather(both, axis, axis=dim, tiled=True)
    return tuple(jnp.split(filled, [sum(widths[:k]) for k in range(1, len(widths))], axis=along))


def rotate(vectors, positions):
    half_width = vectors.shape[-1] // 2
    inv_freq = jnp.exp(
        -(jnp.arange(half_width, dtype=jnp.float32) * (2.0 / vectors.shape[-1]))
        * math.log(500000.0)
    )
    angles = positions.astype(jnp.float32)[:, None] * inv_freq[None, :]
    cosine = jnp.cos(angles)[:, None, :]
    sine = jnp.sin(angles)[:, None, :]
    front_half = vectors[..., :half_width]
    back_half = vectors[..., half_width:]
    return jnp.concatenate(
        [front_half * cosine - back_half * sine, back_half * cosine + front_half * sine], -1
    )


def merge_block(
    states_in, query_heads, query_pos, query_segs, key_part, val_part, key_segs, key_pos
):
    peak_old, totals, weighted = states_in
    scores = jnp.einsum(
        "qkgd,skd->kgqs", query_heads, key_part, preferred_element_type=jnp.float32
    ) * (1.0 / math.sqrt(HEAD_SIZE))
    visible = (key_pos[None, :] <= query_pos[:, None]) & (key_segs[None, :] == query_segs[:, None])
    scores = jnp.where(visible[None, None], scores, -1e30)
    peak_new = jnp.maximum(peak_old, jnp.max(scores, -1))
    probs = jnp.where(visible[None, None], jnp.exp(scores - peak_new[..., None]), 0.0)
    rescale = jnp.exp(peak_old - peak_new)
    totals = totals * rescale + jnp.sum(probs, -1)
    weighted = weighted * rescale[..., None] + jnp.einsum(
        "kgqs,skd->kgqd", probs.astype(jnp.bfloat16), val_part, preferred_element_type=jnp.float32
    )
    return (peak_new, totals, weighted)


def body(tokens, norm_gain, w_query, key_matrix, value_matrix, seg_ids):
    wide_tokens = tokens.astype(jnp.float32)
    rms_normalized = (
        wide_tokens
        * lax.rsqrt(jnp.mean(wide_tokens * wide_tokens, -1, keepdims=True) + 1e-05)
        * norm_gain.astype(jnp.float32)
    ).astype(jnp.bfloat16)
    pieces = lax.all_gather(rms_normalized, "tensor", axis=0, tiled=True)
    projected = jnp.concatenate(
        [
            jnp.dot(pieces, w_query, preferred_element_type=jnp.float32),
            jnp.dot(pieces, key_matrix, preferred_element_type=jnp.float32),
            jnp.dot(pieces, value_matrix, preferred_element_type=jnp.float32),
        ],
        1,
    )
    span_rows = projected.shape[0]
    width_q = w_query.shape[1]
    width_k = key_matrix.shape[1]
    heads_q = width_q // HEAD_SIZE
    heads_kv = width_k // HEAD_SIZE
    heads_per_group = heads_q // heads_kv
    offset = lax.axis_index("context") * span_rows
    positions = offset + jnp.arange(span_rows, dtype=jnp.int32)
    query = rotate(projected[:, :width_q].reshape(span_rows, heads_q, HEAD_SIZE), positions).astype(
        jnp.bfloat16
    )
    key = rotate(
        projected[:, width_q : width_q + width_k].reshape(span_rows, heads_kv, HEAD_SIZE), positions
    ).astype(jnp.bfloat16)
    key = key.reshape(span_rows, width_k)
    value_rows = projected[:, width_q + width_k :].astype(jnp.bfloat16)
    groups = (query, positions, lax.dynamic_slice_in_dim(seg_ids, offset, span_rows, 0))
    query_rows, query_pos, query_segs = groups
    count = query_rows.shape[0]
    prepared = [
        (query_rows.reshape(count, heads_kv, heads_per_group, HEAD_SIZE), query_pos, query_segs)
    ]
    initial = [
        (
            jnp.full((heads_kv, heads_per_group, count), -1e30, jnp.float32),
            jnp.zeros((heads_kv, heads_per_group, count), jnp.float32),
            jnp.zeros((heads_kv, heads_per_group, count, HEAD_SIZE), jnp.float32),
        )
    ]
    states = tuple(initial)
    anchor = jnp.int32(0)
    keys_in, values_in = sent_together((key, value_rows), "context", 0, 1)
    length = keys_in.shape[0]
    sub_rows = math.gcd(length, 512)
    parts_count = length // sub_rows
    key_blocks = keys_in.reshape(parts_count, sub_rows, heads_kv, HEAD_SIZE)
    value_blocks = values_in.reshape(parts_count, sub_rows, heads_kv, HEAD_SIZE)
    key_pos_all = jnp.arange(length, dtype=jnp.int32)
    seg_blocks = seg_ids.reshape(parts_count, sub_rows)
    pos_blocks = key_pos_all.reshape(parts_count, sub_rows)
    results = []
    for (query_heads, query_pos, query_segs), states_in in zip(prepared, states):
        skipped = (anchor > jnp.max(query_pos)) | (seg_ids[length - 1] < jnp.min(query_segs))

        def update(carried, query_heads=query_heads, query_pos=query_pos, query_segs=query_segs):

            def inner(running, slices):
                key_part, val_part, key_segs, key_pos = slices
                return (
                    merge_block(
                        running,
                        query_heads,
                        query_pos,
                        query_segs,
                        key_part,
                        val_part,
                        key_segs,
                        key_pos,
                    ),
                    None,
                )

            return lax.scan(inner, carried, (key_blocks, value_blocks, seg_blocks, pos_blocks))[0]

        results.append(lax.cond(skipped, lambda carried: carried, update, states_in))
    finals = tuple(results)
    outputs = []
    for peak_val, totals, weighted in finals:
        count = weighted.shape[2]
        normalized = weighted / totals[..., None]
        outputs.append(
            jnp.transpose(normalized, (2, 0, 1, 3)).reshape(count, width_q).astype(jnp.bfloat16)
        )
    return outputs[0]


def solution(mesh):
    in_specs = (
        P(("dp", "context", "tensor"), None),
        P(),
        P(None, "tensor"),
        P(None, "tensor"),
        P(None, "tensor"),
        P("dp"),
    )
    out_specs = P(("dp", "context"), "tensor")
    return jax.shard_map(body, mesh=mesh, in_specs=in_specs, out_specs=out_specs, check_vma=False)
```

profile of v0, /device:TPU:6, one launch (start us, length us, event | category | flops | bytes accessed | tf_op | source)
XLA Modules:
  0.0 280.7 jit_solution(2508843274565658553)
XLA Ops:
  10.8 61.8 %all-gather.3.cloned.1.call-done = bf16[512,4096]{1,0:T(8,128)(2,1)} async-done(((bf16[64,4096]{1,0:T(8,128)(2,1)}), bf16[512,4096]{1,0:T(8,128)(2,1)}) %all-gather.3.cloned.1.call-update) | async-done | bytes 4194320 | tf_op jit(solution)/shard_map/all_gather | solution.py:60
  72.6 4.1 %convolution_bitcast_fusion.1 = f32[512,1,128]{0,2,1:T(8,128)S(1)} fusion(bf16[512,4096]{1,0:T(8,128)(2,1)} %all-gather.3.cloned.1.call-done, bf16[4096,128]{1,0:T(8,128)(2,1)} %param.13), kind=kOutput, calls=%fused_computation.37 | convolution fusion | flops 536870912 | bytes 5505024 | tf_op jit(solution)/shard_map/dot_general | solution.py:64
  85.5 3.5 %fusion.44 = f32[512,256]{0,1:T(8,128)S(1)} fusion(bf16[512,4096]{1,0:T(8,128)(2,1)} %all-gather.3.cloned.1.call-done, bf16[4096,256]{1,0:T(8,128)(2,1)S(1)} %copy-done), kind=kOutput, calls=%fused_computation.73 | convolution fusion | flops 1073741824 | bytes 6815744 | tf_op jit(solution)/shard_map/dot_general | solution.py:63
  90.8 67.8 %all-gather.5.cloned.1.call-done = bf16[8192,256]{0,1:T(8,128)(2,1)} async-done(((bf16[512,256]{0,1:T(8,128)(2,1)}), bf16[8192,256]{0,1:T(8,128)(2,1)}) %all-gather.5.cloned.1.call-update) | async-done | bytes 4194320 | tf_op jit(solution)/shard_map/all_gather | solution.py:14
  158.6 114.0 %conditional.1 = (f32[1,2,512]{2,1,0:T(2,128)S(1)}, f32[1,2,512,128]{3,2,1,0:T(8,128)S(1)}) conditional(s32[]{:T(128)} %convert_element_type.47, (bf16[8192,256]{0,1:T(8,128)(2,1)}, s32[8192]{0:T(1024)S(1)}, s32[16,512]{1,0:T(8,128)S(1)}, s32[16,512]{1,0:T(8,128)S(1)}, s32[512]{0:T(512)S(1)}, /*index=5*/s32[512]{0:T(512)S(1)}, ...), branch_computations={%region_3.8_spmd, %region_8.9_spmd} | conditional | flops 276453376 | bytes 34325800 | solution.py:133
  158.6 6.4 %copy.10 = bf16[8192,256]{1,0:T(8,128)(2,1)} copy(bf16[8192,256]{0,1:T(8,128)(2,1)} %get-tuple-element.134) | data formatting | bytes 8388608 | tf_op jit(solution)/shard_map
  165.1 4.5 %fusion.42 = (bf16[8192,128]{1,0:T(8,128)(2,1)}, bf16[8192,128]{1,0:T(8,128)(2,1)}) fusion(bf16[8192,256]{1,0:T(8,128)(2,1)} %copy.10), kind=kLoop, calls=%fused_computation.71 | loop fusion | bytes 8388608 | tf_op jit(solution)/shard_map/split | solution.py:15
  169.5 103.1 %while.14 = (s32[]{:T(128)}, f32[1,2,512]{2,1,0:T(2,128)S(1)}, f32[1,2,512]{2,1,0:T(2,128)S(1)}, f32[1,2,512,128]{3,2,1,0:T(8,128)S(1)}, s32[16,512]{1,0:T(8,128...) while((s32[]{:T(128)}, f32[1,2,512]{2,1,0:T(2,128)S(1)}, ...), condition=%wide.region_7.7_spmd.clone, body=%wide.region_4.6_spmd.clone.sunk | while | flops 276436992 | bytes 17384616 | solution.py:131
  169.9 2.8 fusion.59
  172.7 2.7 fusion.62
  176.3 2.8 fusion.59
  182.7 2.8 fusion.59
  189.2 2.8 fusion.59
  192.0 2.7 fusion.62
  195.6 2.8 fusion.59
  198.4 2.7 fusion.62
  202.1 2.8 fusion.59
  208.5 2.8 fusion.59
  215.0 2.8 fusion.59
  217.8 2.7 fusion.62
  221.4 2.8 fusion.59
  224.2 2.7 fusion.62
  227.8 2.8 fusion.59
  234.3 2.8 fusion.59
  237.1 2.7 fusion.62
  240.7 2.8 fusion.59
  243.5 2.7 fusion.62
  247.2 2.8 fusion.59
  250.0 2.7 fusion.62
  253.6 2.8 fusion.59
  260.1 2.8 fusion.59
  266.5 2.8 fusion.59
  (177 shorter events, 50.0 us)
Async XLA Ops:
  6.5 79.0 %copy-start = (bf16[4096,256]{1,0:T(8,128)(2,1)S(1)}, bf16[4096,256]{1,0:T(8,128)(2,1)}, u32[]{:S(2)}) copy-start(bf16[4096,256]{1,0:T(8,128)(2,1)} %param.12) | copy-start | bytes 6291460
  6.5 66.1 %all-gather.3.cloned.1.call-start = ((), (), s32[]{:S(2)}) async-start(), calls=%async_computation | async-start | bytes 4718592 | tf_op jit(solution)/shard_map/all_gather | solution.py:60
  10.7 147.9 %all-gather.5.cloned.1.call-start = ((), (), s32[]{:S(2)}) async-start(), calls=%async_computation.1 | async-start | bytes 4456448 | tf_op jit(solution)/shard_map/all_gather | solution.py:14
  10.8 66.5 %copy-start.3 = (bf16[4096,128]{1,0:T(8,128)(2,1)S(1)}, bf16[4096,128]{1,0:T(8,128)(2,1)}, u32[]{:S(2)}) copy-start(bf16[4096,128]{1,0:T(8,128)(2,1)} %param.14) | copy-start | bytes 3145732
  72.6 4.7 %copy-start.2 = (bf16[512,4096]{1,0:T(8,128)(2,1)S(1)}, bf16[512,4096]{1,0:T(8,128)(2,1)}, u32[]{:S(2)}) copy-start(bf16[512,4096]{1,0:T(8,128)(2,1)} %all-gather.3.cloned.1.call-done) | copy-start | bytes 12582916
  77.3 3.0 %copy-start.4 = (s32[8192]{0:T(1024)S(1)}, s32[8192]{0:T(1024)}, u32[]{:S(2)}) copy-start(s32[8192]{0:T(1024)} %param.15) | copy-start | bytes 98308
  172.7 2.7 copy-start.1
  179.1 2.7 copy-start.1
  185.5 2.7 copy-start.1
  192.0 2.7 copy-start.1
  198.4 2.7 copy-start.1
  204.9 2.7 copy-start.1
  211.3 2.7 copy-start.1
  217.8 2.7 copy-start.1
  224.2 2.7 copy-start.1
  230.6 2.7 copy-start.1
  237.1 2.7 copy-start.1
  243.5 2.7 copy-start.1
  250.0 2.7 copy-start.1
  256.4 2.7 copy-start.1
  262.8 2.7 copy-start.1
  269.3 2.7 copy-start.1
Sparse Core Ops, SparseCore 0:
  10.8 61.7 all-gather.2
  79.7 78.8 all-gather.4
where the time goes:
time: 282 us; the launch traced here: 281 us
  waiting for transfers between devices  130 us (46%)
  matrix products  96.7 us (34%)
  other arithmetic  24.4 us (9%)
  between operations  15.6 us (6%)
  local copies, waits for them, and re-layouts  13.3 us (5%)
    all_gather x1, waiting for transfers between devices, sent_together(): filled = lax.all_gather(both, axis, axis=dim, tiled=True)  67.8 us
    all_gather x1, waiting for transfers between devices, body(): pieces = lax.all_gather(rms_normalized, 'tensor', axis=0, tiled=True)  61.8 us
    dot_general x16, matrix products, merge_block(): jnp.einsum('qkgd,skd->kgqs', query_heads, key_part, preferred_element_typ...  44.4 us
    dot_general x16, matrix products, merge_block(): jnp.einsum('kgqs,skd->kgqd', probs.astype(jnp.bfloat16), val_part, prefer...  43.2 us
    reduce_sum x16, other arithmetic, merge_block(): totals = totals * rescale + jnp.sum(probs, -1)  9.2 us
    another operation x1, local copies, waits for them, and re-layouts  6.43 us
  transfers between devices with their start and end apart: 2, of which 2 were waited for; matrix products, arithmetic and copies ran while one was open for 3% of the time, Pallas kernels for 0%

commit v1 on v0

v1 whole, which is shorter than its diff:
```python
import functools
import math

import jax
import jax.numpy as jnp
import numpy as np
from jax import lax
from jax.experimental import pallas as pl
from jax.experimental.pallas import tpu as pltpu
from jax.sharding import PartitionSpec as P

HEAD = 128
MESH = pl.DeviceIdType.MESH
OFFSETS = (0, -1, 1, -2, 2, -3, 3, 4)
DOCS = 8
NEG = -(2.0**100)
LOW = -(2.0**99)
STEPS = ((0, 1), (1, 3), (3, 5), (5, 7), (7, 8))
TILE = 256


def kernel(
    sub,
    reach,
    nctx,
    nten,
    tok,
    gain,
    wq,
    wk,
    wv,
    seg,
    ctab,
    stab,
    atab,
    out,
    x,
    w,
    nrm,
    q,
    kv,
    kaug,
    lp,
    cosv,
    sinv,
    ct,
    st,
    at,
    gv,
    sv,
    acc,
    mx,
    tot,
    local_sem,
    rs_send,
    rs_recv,
    ls_send,
    ls_recv,
    own_send_sem,
    fwd_sem,
    kv_recv,
):
    f32, bf16 = jnp.float32, jnp.bfloat16
    rows = sub * nten
    half = sub // 2
    c = lax.axis_index("context")
    t = lax.axis_index("tensor")
    right = lax.rem(t + 1, nten)
    left = lax.rem(t + nten - 1, nten)
    last = nctx - 1
    wide_q = wq.shape[1]
    heads = wide_q // HEAD

    loads = [
        pltpu.make_async_copy(tok, x.at[pl.ds(0, sub)], local_sem.at[0]),
        pltpu.make_async_copy(seg, sv, local_sem.at[1]),
        pltpu.make_async_copy(gain, gv, local_sem.at[2]),
        pltpu.make_async_copy(atab, at, local_sem.at[3]),
        pltpu.make_async_copy(ctab, ct, local_sem.at[4]),
        pltpu.make_async_copy(stab, st, local_sem.at[5]),
        pltpu.make_async_copy(wq, w.at[:, pl.ds(0, wide_q)], local_sem.at[6]),
        pltpu.make_async_copy(wk, w.at[:, pl.ds(wide_q, HEAD)], local_sem.at[7]),
        pltpu.make_async_copy(wv, w.at[:, pl.ds(wide_q + HEAD, HEAD)], local_sem.at[8]),
    ]
    for one in loads:
        one.start()

    barrier = pltpu.get_barrier_semaphore()

    def greet(where):
        pl.semaphore_signal(barrier, inc=1, device_id=where, device_id_type=MESH)

    greet({"tensor": left})
    greet({"tensor": right})

    @pl.when(c >= 1)
    def _():
        greet({"context": c - 1})

    @pl.when(c < last)
    def _():
        greet({"context": c + 1})

    @pl.when(c >= reach)
    def _():
        greet({"context": c - reach})

    @pl.when(c + reach <= last)
    def _():
        greet({"context": c + reach})

    tails = [last - d for d in range(5, reach)]
    for s in tails:

        @pl.when(c == s)
        def _():
            greet({"context": last})

        @pl.when(c == last)
        def _(s=s):
            greet({"context": s})

    one = jnp.int32(1)
    zero = jnp.int32(0)
    expected = (
        2
        + jnp.where(c >= 1, one, zero)
        + jnp.where(c < last, one, zero)
        + jnp.where(c >= reach, one, zero)
        + jnp.where(c + reach <= last, one, zero)
        + jnp.where(c == last, jnp.int32(len(tails)), zero)
    )
    for s in tails:
        expected = expected + jnp.where(c == s, one, zero)
    pl.semaphore_wait(barrier, expected)

    def half_rows(slot, which):
        return pl.ds(slot * sub + which * half, half)

    def ring_copy(k, to_right):
        first = 0 if to_right else 1
        which = first if k % 2 == 0 else 1 - first
        hop = k // 2
        odd = 1 if to_right else 2
        if hop == 0:
            src = tok.at[pl.ds(which * half, half)]
        else:
            src = x.at[half_rows(2 * (hop - 1) + odd, which)]
        slot = 2 * hop + odd if hop < 3 else 7
        return pltpu.make_async_remote_copy(
            src_ref=src,
            dst_ref=x.at[half_rows(slot, which)],
            send_sem=(rs_send if to_right else ls_send).at[k],
            recv_sem=(rs_recv if to_right else ls_recv).at[k],
            device_id={"tensor": right if to_right else left},
            device_id_type=MESH,
        )

    for k in (0, 1):
        ring_copy(k, True).start()
        ring_copy(k, False).start()

    def ring_step(k):
        ring_copy(k, True).wait_recv()
        if k <= 4:
            ring_copy(k + 2, True).start()
        ring_copy(k, False).wait_recv()
        if k <= 4:
            ring_copy(k + 2, False).start()

    def part(m):
        lo, hi = STEPS[m]
        return pl.ds(lo * sub, (hi - lo) * sub)

    def kv_copy(m, src_slot, dst_slot, target, sem, recv):
        return pltpu.make_async_remote_copy(
            src_ref=kv.at[src_slot, part(m)],
            dst_ref=kv.at[dst_slot, part(m)],
            send_sem=sem,
            recv_sem=recv,
            device_id={"context": target},
            device_id_type=MESH,
        )

    def own_copies(m):
        res = [(c < last, kv_copy(m, 0, 1, c + 1, own_send_sem.at[0, m], kv_recv.at[1, m]))]
        res.append(
            (
                c + reach <= last,
                kv_copy(m, 0, reach, c + reach, own_send_sem.at[1, m], kv_recv.at[reach, m]),
            )
        )
        for d in range(5, reach):
            res.append(
                (c == last - d, kv_copy(m, 0, d, last, own_send_sem.at[1, m], kv_recv.at[d, m]))
            )
        return res

    def own_send(m):
        for cond, copy in own_copies(m):

            @pl.when(cond)
            def _(copy=copy):
                copy.start()

    def forward(m, d):
        if d <= 3:
            return (
                (c >= d) & (c < last),
                kv_copy(m, d, d + 1, c + 1, fwd_sem.at[d, m], kv_recv.at[d + 1, m]),
            )
        if d >= 6:
            return (
                c >= d,
                kv_copy(m, d, d - 1, c - 1, fwd_sem.at[d, m], kv_recv.at[d - 1, m]),
            )
        return None

    def relay(m, d):
        @pl.when(c >= d)
        def _():
            kv_copy(m, d, d, c, fwd_sem.at[d, m], kv_recv.at[d, m]).wait_recv()

        f = forward(m, d)
        if f is not None:

            @pl.when(f[0])
            def _():
                f[1].start()

    def hop(m, h):
        relay(m, h)
        relay(m, reach + 1 - h)

    lane = lax.broadcasted_iota(jnp.int32, (1, HEAD), 1)
    places = [lax.rem(t + o + nten, nten) * sub for o in OFFSETS]
    for a in range(nten):
        lp[a * sub : (a + 1) * sub, :] = (
            places[a] + lax.broadcasted_iota(jnp.int32, (sub, HEAD), 0)
        ).astype(f32)
    for i in (1, 3, 4, 5):
        loads[i].wait()
    total_rows = nctx * rows
    segv = sv[...]
    begin = jnp.where(lane >= DOCS, f32(total_rows), f32(0.0))
    end = jnp.full((1, HEAD), total_rows, f32)
    for e in range(1, DOCS):
        count = jnp.sum(jnp.where(segv < e, f32(1.0), f32(0.0)))
        begin = jnp.where(lane == e, count, begin)
        end = jnp.where(lane == e - 1, count, end)
    for d in range(reach + 1):
        base = ((c - d) * rows).astype(f32)

        @pl.when(c >= d)
        def _():
            here = lp[...] + base
            kaug[d] = jnp.where((here >= begin) & (here < end), f32(1.0), f32(0.0)).astype(bf16)

    qaug = jnp.where(kaug[0].astype(f32) > 0.5, f32(0.0), f32(NEG)).astype(bf16)
    for h in range(heads):
        q[h * rows : (h + 1) * rows, HEAD : 2 * HEAD] = qaug
    mine = lax.broadcasted_iota(jnp.int32, (nctx, 2 * HEAD), 0) == c
    both = jnp.sum(jnp.where(mine, at[...], 0.0), 0, keepdims=True)
    ca, sa = both[:, 0:HEAD], both[:, HEAD : 2 * HEAD]
    sign = jnp.where(lane < HEAD // 2, f32(-1.0), f32(1.0))
    for a in range(nten):
        here = pl.ds(pl.multiple_of(places[a], sub), sub)
        cb, sb = ct[here, :], st[here, :]
        cosv[a * sub : (a + 1) * sub, :] = ca * cb - sa * sb
        sinv[a * sub : (a + 1) * sub, :] = (sa * cb + ca * sb) * sign

    def project(m):
        lo, hi = STEPS[m]
        r0, n = lo * sub, (hi - lo) * sub

        def norm(i, carry):
            v = x[pl.ds(r0 + i * 16, 16), :].astype(f32)
            mean = jnp.sum(v * v, -1, keepdims=True) * (1.0 / v.shape[1])
            nrm[pl.ds(i * 16, 16), :] = (v * lax.rsqrt(mean + 1e-05) * gv[...].astype(f32)).astype(
                bf16
            )
            return carry

        lax.fori_loop(0, n // 16, norm, 0)
        got = jnp.dot(nrm[0:n, :], w[...], preferred_element_type=f32)
        cs, sn = cosv[r0 : r0 + n, :], sinv[r0 : r0 + n, :]

        def rotate(v):
            return (v * cs + pltpu.roll(v, HEAD // 2, 1) * sn).astype(bf16)

        for h in range(heads):
            q[h * rows + r0 : h * rows + r0 + n, 0:HEAD] = rotate(got[:, h * HEAD : (h + 1) * HEAD])
        kv[0, r0 : r0 + n, 0:HEAD] = rotate(got[:, wide_q : wide_q + HEAD])
        kv[0, r0 : r0 + n, HEAD : 2 * HEAD] = got[:, wide_q + HEAD :].astype(bf16)

    scale = math.log2(math.e) / math.sqrt(HEAD)
    acc[...] = jnp.zeros_like(acc)
    tot[...] = jnp.zeros_like(tot)
    mx[...] = jnp.full_like(mx, LOW)
    col = lax.broadcasted_iota(jnp.int32, (1, rows), 1)
    kpos = jnp.zeros((1, rows), jnp.int32)
    for a in range(nten):
        kpos = jnp.where((col >= a * sub) & (col < (a + 1) * sub), places[a] + col - a * sub, kpos)
    kpos = kpos.astype(f32)

    def attend(d):
        @pl.when(c >= d)
        def _():
            keys = jnp.concatenate([kv[d, :, 0:HEAD], kaug[d]], 1)
            vals = kv[d, :, HEAD : 2 * HEAD]
            for i in range(heads * rows // TILE):
                at_rows = slice(i * TILE, (i + 1) * TILE)
                s = (
                    lax.dot_general(
                        q[at_rows, :], keys, (((1,), (1,)), ((), ())), preferred_element_type=f32
                    )
                    * scale
                )
                if d == 0:
                    r = (i * TILE) % rows
                    s = jnp.where(kpos <= lp[r : r + TILE, 0:1], s, NEG)
                old = mx[at_rows, 0:1]
                new = jnp.maximum(old, jnp.max(s, -1, keepdims=True))
                p = jnp.exp2(s - new)
                fade = jnp.exp2(old - new)
                mx[at_rows, 0:1] = new
                tot[at_rows, 0:1] = tot[at_rows, 0:1] * fade + jnp.sum(p, -1, keepdims=True)
                acc[at_rows, :] = acc[at_rows, :] * fade + jnp.dot(
                    p.astype(bf16), vals, preferred_element_type=f32
                )

    for i in (0, 2, 6, 7, 8):
        loads[i].wait()
    project(0)
    own_send(0)
    ring_step(0)
    hop(0, 1)
    ring_step(1)
    project(1)
    own_send(1)
    hop(0, 2)
    ring_step(2)
    hop(0, 3)
    hop(1, 1)
    ring_step(3)
    project(2)
    own_send(2)
    hop(0, 4)
    hop(1, 2)
    ring_step(4)
    hop(1, 3)
    hop(2, 1)
    ring_step(5)
    project(3)
    own_send(3)
    hop(1, 4)
    hop(2, 2)
    hop(2, 3)
    hop(2, 4)
    hop(3, 1)
    hop(3, 2)
    hop(3, 3)
    ring_step(6)
    project(4)
    own_send(4)
    hop(3, 4)
    attend(0)
    for h in range(1, 5):
        hop(4, h)
        attend(h)
        attend(reach + 1 - h)

    for h in range(heads):
        for a in range(nten):
            r = h * rows + a * sub
            done = acc[r : r + sub, :] / tot[r : r + sub, 0:1]
            out[pl.ds(pl.multiple_of(places[a], sub), sub), h * HEAD : (h + 1) * HEAD] = (
                done.astype(bf16)
            )

    for k in range(7):
        ring_copy(k, True).wait_send()
        ring_copy(k, False).wait_send()
    for m in range(len(STEPS)):
        waits = own_copies(m) + [forward(m, d) for d in (1, 2, 3, 6, 7, 8)]
        for cond, copy in waits:

            @pl.when(cond)
            def _(copy=copy):
                copy.wait_send()


def tables(rows, nctx):
    freq = np.exp(-(np.arange(HEAD // 2) * (2.0 / HEAD)) * math.log(500000.0))
    fine = np.arange(rows)[:, None] * freq[None, :]
    coarse = (np.arange(nctx) * rows)[:, None] * freq[None, :]
    twice = lambda v: np.concatenate([v, v], 1).astype(np.float32)
    both = np.concatenate([twice(np.cos(coarse)), twice(np.sin(coarse))], 1)
    return twice(np.cos(fine)), twice(np.sin(fine)), both


def solution(mesh):
    nctx, nten = mesh.shape["context"], mesh.shape["tensor"]

    def body(tokens, norm_gain, w_query, key_matrix, value_matrix, seg_ids):
        sub, width = tokens.shape
        rows = sub * nten
        wide_q = w_query.shape[1]
        heads = wide_q // HEAD
        reach = 4096 // rows
        ctab, stab, atab = tables(rows, nctx)

        hbm = pl.BlockSpec(memory_space=pl.ANY)
        dma = pltpu.SemaphoreType.DMA
        f32, bf16 = jnp.float32, jnp.bfloat16
        return pl.pallas_call(
            functools.partial(kernel, sub, reach, nctx, nten),
            out_shape=jax.ShapeDtypeStruct((rows, wide_q), bf16),
            in_specs=[hbm] * 9,
            out_specs=pl.BlockSpec(memory_space=pltpu.VMEM),
            scratch_shapes=[
                pltpu.VMEM((rows, width), bf16),
                pltpu.VMEM((width, wide_q + 2 * HEAD), bf16),
                pltpu.VMEM((2 * sub, width), bf16),
                pltpu.VMEM((heads * rows, 2 * HEAD), bf16),
                pltpu.VMEM((reach + 1, rows, 2 * HEAD), bf16),
                pltpu.VMEM((reach + 1, rows, HEAD), bf16),
                pltpu.VMEM((rows, HEAD), f32),
                pltpu.VMEM((rows, HEAD), f32),
                pltpu.VMEM((rows, HEAD), f32),
                pltpu.VMEM((rows, HEAD), f32),
                pltpu.VMEM((rows, HEAD), f32),
                pltpu.VMEM((nctx, 2 * HEAD), f32),
                pltpu.VMEM((1, width), bf16),
                pltpu.VMEM((seg_ids.shape[0] // HEAD, HEAD), jnp.int32),
                pltpu.VMEM((heads * rows, HEAD), f32),
                pltpu.VMEM((heads * rows, HEAD), f32),
                pltpu.VMEM((heads * rows, HEAD), f32),
                dma((9,)),
                dma((7,)),
                dma((7,)),
                dma((7,)),
                dma((7,)),
                dma((2, len(STEPS))),
                dma((reach + 1, len(STEPS))),
                dma((reach + 1, len(STEPS))),
            ],
            compiler_params=pltpu.CompilerParams(
                collective_id=0, has_side_effects=True, vmem_limit_bytes=60 << 20
            ),
        )(
            tokens,
            norm_gain.reshape(1, width),
            w_query,
            key_matrix,
            value_matrix,
            seg_ids.reshape(-1, HEAD),
            ctab,
            stab,
            atab,
        )

    in_specs = (
        P(("dp", "context", "tensor"), None),
        P(),
        P(None, "tensor"),
        P(None, "tensor"),
        P(None, "tensor"),
        P("dp"),
    )
    out_specs = P(("dp", "context"), "tensor")
    return jax.shard_map(body, mesh=mesh, in_specs=in_specs, out_specs=out_specs, check_vma=False)
```

time: 282 us -> 96.4 us (0.34)
  waiting for transfers between devices: 130 us -> 0 us
  matrix products: 96.7 us -> 0 us
  Pallas kernels: 0 us -> 93.2 us
  other arithmetic: 24.4 us -> 0 us
  between operations: 15.6 us -> 0.01 us
  local copies, waits for them, and re-layouts: 13.3 us -> 2.98 us
    all_gather x2 -> x0, waiting for transfers between devices: 130 us -> none  [the longest x1 67.8 us: sent_together(): filled = lax.all_gather(both, axis, axis=dim, tiled=True)]
    dot_general x35 -> x0, matrix products: 96.7 us -> none  [the longest x16 44.4 us: merge_block(): jnp.einsum('qkgd,skd->kgqs', query_heads, key_part, preferred_element_typ...]
    pallas_call x0 -> x1, Pallas kernels: none -> 93.2 us  [body(): pl.pallas_call(functools.partial(kernel, sub, reach, nctx, nten), out_sha...]
    reduce_sum x17 -> x0, other arithmetic: 10.4 us -> none  [the longest x16 9.2 us: merge_block(): totals = totals * rescale + jnp.sum(probs, -1)]
    another operation x1 -> x0, local copies, waits for them, and re-layouts: 6.43 us -> none
    split x1 -> x0, local copies, waits for them, and re-layouts: 4.45 us -> none  [sent_together(): jnp.split(filled, [sum(widths[:k]) for k in range(1, len(widths))], axis=...]
    and x16 -> x0, other arithmetic: 4.42 us -> none  [merge_block(): (key_pos[None, :] <= query_pos[:, None]) & (key_segs[None, :] == query_se...]
    convert_element_type x4 -> x0, other arithmetic: 3.1 us -> none  [the longest x1 2.04 us: body(): rms_normalized = (wide_tokens * lax.rsqrt(jnp.mean(wide_tokens * wide_tok...]
  transfers between devices with their start and end apart: 2 -> 0, of which waited for: 2 -> 0; matrix products, arithmetic and copies ran while one was open for 3% -> 0% of each run, Pallas kernels for 0% -> 0%
where the time goes in v1:
time: 96.4 us; the launch traced here: 96.2 us
  Pallas kernels  93.2 us (97%)
  local copies, waits for them, and re-layouts  2.98 us (3%)
    pallas_call x1, Pallas kernels, body(): pl.pallas_call(functools.partial(kernel, sub, reach, nctx, nten), out_sha...  93.2 us

profile of v1, /device:TPU:6, one launch (start us, length us, event | category | flops | bytes accessed | tf_op | source)
XLA Modules:
  0.0 96.2 jit_solution(11652013245863389726)
XLA Ops:
  0.0 1.3 %reshape.6.gain = bf16[1,4096]{1,0:T(2,128)(2,1)} reshape(bf16[4096]{0:T(1024)(128)(2,1)} %param.10) | data formatting | bytes 16384 | tf_op jit(solution)/shard_map/reshape | solution.py:453
  1.3 93.2 %shard_map.91 = bf16[512,256]{1,0:T(8,128)(2,1)} custom-call(bf16[64,4096]{1,0:T(8,128)(2,1)} %tok.1, bf16[1,4096]{1,0:T(2,128)(2,1)} %reshape.6.gain, bf16[4096,256]{1,0:T(8,128)(2,1)} %wq.1, bf16[4096,128]{1,0:T(8,128)(2,1)} %wk.1, bf16[4096,128]{1,0:T(8,128)(2,1)} %wv.1, s32[64,128]{1,0:T(8,128)} %bitcast.1, f32[512,128]{1,0:T(8,128)} %constant.6.clone.ctab, ...), custom_call_target="tpu_custom_call" | custom-call | tf_op jit(solution)/shard_map/pallas_call | solution.py:416
  94.6 1.7 %copy.11 = bf16[512,256]{1,0:T(8,128)(2,1)} copy(bf16[512,256]{1,0:T(8,128)(2,1)} %shard_map.91) | data formatting | bytes 524288

commit v2 on v1

v2 whole, which is shorter than its diff:
```python
import functools
import math

import jax
import jax.numpy as jnp
import numpy as np
from jax import lax
from jax.experimental import pallas as pl
from jax.experimental.pallas import tpu as pltpu
from jax.sharding import PartitionSpec as P

HEAD = 128
MESH = pl.DeviceIdType.MESH
DOCS = 8
NEG = -(2.0**100)
LOW = -(2.0**99)
ARRIVAL = [(0, 0), (0, 1)]
for _k in range(7):
    ARRIVAL += [(-(1 + _k // 2), _k % 2), (1 + _k // 2, 1 - _k % 2)]
DIRECT = (1, 2, 7, 8)
PASSED = {2: ((1, 3), (2, 4)), 7: ((-1, 6), (-2, 5))}
EXTRA = ((6, 6), (6, 5), (5, 5))
WAITED = (1, 3, 4, 5, 6, 8)
RING = PROJ = KV = ATT = True


def kernel(
    sub,
    reach,
    nctx,
    nten,
    tok,
    gain,
    wq,
    wk,
    wv,
    seg,
    ctab,
    stab,
    atab,
    out,
    x,
    w,
    nrm,
    q,
    kv,
    kaug,
    lp,
    qp,
    kp,
    cosv,
    sinv,
    ct,
    st,
    at,
    gv,
    sv,
    acc,
    mx,
    tot,
    local_sem,
    rs_send,
    rs_recv,
    ls_send,
    ls_recv,
    own_sem,
    fwd_sem,
    kv_recv,
):
    f32, bf16 = jnp.float32, jnp.bfloat16
    rows = sub * nten
    half = sub // 2
    c = lax.axis_index("context")
    t = lax.axis_index("tensor")
    right = lax.rem(t + 1, nten)
    left = lax.rem(t + nten - 1, nten)
    last = nctx - 1
    wide_q = wq.shape[1]
    heads = wide_q // HEAD
    msgs = nten
    slots = reach + 1
    tile = heads * sub

    loads = [
        pltpu.make_async_copy(tok, x.at[pl.ds(0, sub)], local_sem.at[0]),
        pltpu.make_async_copy(seg, sv, local_sem.at[1]),
        pltpu.make_async_copy(gain, gv, local_sem.at[2]),
        pltpu.make_async_copy(atab, at, local_sem.at[3]),
        pltpu.make_async_copy(ctab, ct, local_sem.at[4]),
        pltpu.make_async_copy(stab, st, local_sem.at[5]),
        pltpu.make_async_copy(wq, w.at[:, pl.ds(0, wide_q)], local_sem.at[6]),
        pltpu.make_async_copy(wk, w.at[:, pl.ds(wide_q, HEAD)], local_sem.at[7]),
        pltpu.make_async_copy(wv, w.at[:, pl.ds(wide_q + HEAD, HEAD)], local_sem.at[8]),
    ]

    barrier = pltpu.get_barrier_semaphore()
    one, zero = jnp.int32(1), jnp.int32(0)
    links = [(c >= d, c - d) for d in DIRECT] + [(c + d <= last, c + d) for d in DIRECT]
    for back, d in EXTRA:
        links.append((c == last - back, c + d))
        links.append((c == last - back + d, c - d))
    for where in (left, right):
        pl.semaphore_signal(barrier, inc=1, device_id={"tensor": where}, device_id_type=MESH)
    expected = jnp.int32(2)
    for cond, where in links:

        @pl.when(cond)
        def _(where=where):
            pl.semaphore_signal(barrier, inc=1, device_id={"context": where}, device_id_type=MESH)

        expected = expected + jnp.where(cond, one, zero)
    for load in loads:
        load.start()
    pl.semaphore_wait(barrier, expected)

    def unit(u):
        return x.at[pl.ds(u * half, half)]

    def ring_copy(k, to_right):
        first = 2 if to_right else 3
        if k < 2:
            src = tok.at[pl.ds((k if to_right else 1 - k) * half, half)]
        else:
            src = unit(first + 2 * (k - 2))
        return pltpu.make_async_remote_copy(
            src_ref=src,
            dst_ref=unit(first + 2 * k),
            send_sem=(rs_send if to_right else ls_send).at[k],
            recv_sem=(rs_recv if to_right else ls_recv).at[k],
            device_id={"tensor": right if to_right else left},
            device_id_type=MESH,
        )

    def ring_step(k):
        for to_right in (True, False):
            ring_copy(k, to_right).wait_recv()
            if k <= 4:
                ring_copy(k + 2, to_right).start()

    def kv_copy(m, src_slot, dst_slot, target, sem):
        return pltpu.make_async_remote_copy(
            src_ref=kv.at[m, pl.ds(src_slot * sub, sub)],
            dst_ref=kv.at[m, pl.ds(dst_slot * sub, sub)],
            send_sem=sem,
            recv_sem=kv_recv.at[dst_slot, m],
            device_id={"context": target},
            device_id_type=MESH,
        )

    def own_copies(m):
        res = [
            (c + d <= last, kv_copy(m, 0, d, c + d, own_sem.at[i, m])) for i, d in enumerate(DIRECT)
        ]
        for back, d in EXTRA:
            res.append((c == last - back, kv_copy(m, 0, d, c + d, own_sem.at[d - 3, m])))
        return res

    def passed_copies(m, slot):
        first = 0 if slot == 2 else 2
        return [
            (
                (c >= slot) & (c + step <= last),
                kv_copy(m, slot, there, c + step, fwd_sem.at[first + i, m]),
            )
            for i, (step, there) in enumerate(PASSED[slot])
        ]

    def start_all(copies):
        for cond, copy in copies:

            @pl.when(cond)
            def _(copy=copy):
                copy.start()

    def landed(m, d):
        @pl.when(c >= d)
        def _():
            kv_copy(m, d, d, c, own_sem.at[0, m]).wait_recv()

    def own_send(m):
        start_all(own_copies(m))

    def relay(m):
        for slot in PASSED:
            landed(m, slot)
            start_all(passed_copies(m, slot))

    def arrived(m):
        for d in WAITED:
            landed(m, d)

    if RING:
        for k in (0, 1):
            ring_copy(k, True).start()
            ring_copy(k, False).start()

    lane = lax.broadcasted_iota(jnp.int32, (1, HEAD), 1)
    places = [lax.rem(t + o + nten, nten) * sub + h * half for o, h in ARRIVAL]
    for u in range(2 * nten):
        spot = (places[u] + lax.broadcasted_iota(jnp.int32, (half, HEAD), 0)).astype(f32)
        lp[u * half : (u + 1) * half, :] = spot
        for h in range(heads):
            r = (u // 2) * tile + h * sub + (u % 2) * half
            qp[r : r + half, :] = spot
    for i in (1, 3, 4, 5):
        loads[i].wait()
    total_rows = nctx * rows
    segv = sv[...]
    begin = jnp.where(lane >= DOCS, f32(total_rows), f32(0.0))
    end = jnp.full((1, HEAD), total_rows, f32)
    for e in range(1, DOCS):
        count = jnp.sum(jnp.where(segv < e, f32(1.0), f32(0.0)))
        begin = jnp.where(lane == e, count, begin)
        end = jnp.where(lane == e - 1, count, end)
    begin = jnp.where(lane == DOCS, f32(-total_rows), begin)
    end = jnp.where(lane == DOCS, f32(0.0), end)
    missing = jnp.where(lane == DOCS, f32(1.0), f32(0.0)).astype(bf16)
    mine = lax.broadcasted_iota(jnp.int32, (nctx, 2 * HEAD), 0) == c
    both = jnp.sum(jnp.where(mine, at[...], 0.0), 0, keepdims=True)
    ca, sa = both[:, 0:HEAD], both[:, HEAD : 2 * HEAD]
    sign = jnp.where(lane < HEAD // 2, f32(-1.0), f32(1.0))
    for u in range(2 * nten):
        here = pl.ds(pl.multiple_of(places[u], half), half)
        cb, sb = ct[here, :], st[here, :]
        cosv[u * half : (u + 1) * half, :] = ca * cb - sa * sb
        sinv[u * half : (u + 1) * half, :] = (sa * cb + ca * sb) * sign

    def masks(m, carry):
        local = lp[pl.ds(pl.multiple_of(m * sub, sub), sub), :]
        for d in range(slots):
            here = local + ((c - d) * rows).astype(f32)
            kaug[m, d * sub : (d + 1) * sub, :] = jnp.where(
                (here >= begin) & (here < end), f32(1.0), f32(0.0)
            ).astype(bf16)
        kaug[m, slots * sub :, :] = jnp.broadcast_to(missing, (kaug.shape[1] - slots * sub, HEAD))
        kv[m, slots * sub :, :] = jnp.zeros((kv.shape[1] - slots * sub, 2 * HEAD), bf16)
        qaug = jnp.where(kaug[m, 0:sub, :].astype(f32) > 0.5, f32(0.0), f32(NEG)).astype(bf16)
        for h in range(heads):
            r = pl.multiple_of(m * tile + h * sub, sub)
            q[pl.ds(r, sub), HEAD : 2 * HEAD] = qaug
        for d in range(1, slots):

            @pl.when(c < d)
            def _():
                kv[m, d * sub : (d + 1) * sub, :] = jnp.zeros((sub, 2 * HEAD), bf16)

        return carry

    lax.fori_loop(0, msgs, masks, 0)
    for m in range(msgs):
        spot = jnp.where(
            lane < half,
            places[2 * m] + lane,
            jnp.where(lane < sub, places[2 * m + 1] + lane - half, -1),
        ).astype(f32)
        kp[m] = jnp.broadcast_to(spot, (8, HEAD))
    acc[...] = jnp.zeros_like(acc)
    tot[...] = jnp.zeros_like(tot)
    mx[...] = jnp.full_like(mx, LOW)

    scale = math.log2(math.e) / math.sqrt(HEAD)

    def project(m):
        r0 = m * sub

        def norm(i, carry):
            v = x[pl.ds(r0 + i * 16, 16), :].astype(f32)
            mean = jnp.sum(v * v, -1, keepdims=True) * (1.0 / v.shape[1])
            nrm[pl.ds(i * 16, 16), :] = (v * lax.rsqrt(mean + 1e-05) * gv[...].astype(f32)).astype(
                bf16
            )
            return carry

        lax.fori_loop(0, sub // 16, norm, 0)
        got = jnp.dot(nrm[...], w[...], preferred_element_type=f32)
        cs, sn = cosv[r0 : r0 + sub, :], sinv[r0 : r0 + sub, :]

        def rotate(v):
            return v * cs + pltpu.roll(v, HEAD // 2, 1) * sn

        kv[m, 0:sub, 0:HEAD] = rotate(got[:, wide_q : wide_q + HEAD]).astype(bf16)
        kv[m, 0:sub, HEAD : 2 * HEAD] = got[:, wide_q + HEAD :].astype(bf16)
        for h in range(heads):
            r = m * tile + h * sub
            q[r : r + sub, 0:HEAD] = (rotate(got[:, h * HEAD : (h + 1) * HEAD]) * scale).astype(bf16)

    chunks = kv.shape[1] // HEAD

    def attend_rows(here, j):
        keys = jnp.concatenate([kv[j, :, 0:HEAD], kaug[j]], 1)
        vals = kv[j, :, HEAD : 2 * HEAD]
        s = lax.dot_general(
            q[here, :], keys, (((1,), (1,)), ((), ())), preferred_element_type=f32
        )
        cols = [s[:, i * HEAD : (i + 1) * HEAD] for i in range(chunks)]
        cols[0] = jnp.where(kp[j][0:1, :] <= qp[here, :], cols[0], NEG)
        old = mx[here, :]
        top = functools.reduce(jnp.maximum, cols)
        new = jnp.maximum(old, jnp.max(top, -1, keepdims=True))
        p = [jnp.exp2(v - new) for v in cols]
        fade = jnp.exp2(old - new)
        mx[here, :] = new
        tot[here, :] = tot[here, :] * fade + functools.reduce(jnp.add, p)
        low = jnp.concatenate([v.astype(bf16) for v in p], 1)
        acc[here, :] = acc[here, :] * fade + jnp.dot(low, vals, preferred_element_type=f32)

    def attend(lo, hi, j):
        pairs = (hi - lo) // 2

        def two(i, carry):
            r = pl.multiple_of(lo * tile + i * 2 * tile, tile)
            attend_rows(pl.ds(r, 2 * tile), j)
            return carry

        if pairs:
            lax.fori_loop(0, pairs, two, 0)
        if (hi - lo) % 2:
            attend_rows(pl.ds((hi - 1) * tile, tile), j)

    def attend_keys(i, lo, hi):
        def step(j, carry):
            attend_rows(pl.ds(i * tile, tile), j)
            return carry

        if hi > lo:
            lax.fori_loop(lo, hi, step, 0)

    for i in (0, 2, 6, 7, 8):
        loads[i].wait()
    for s in range(msgs):
        if RING and s >= 1:
            ring_step(s - 1)
        if PROJ:
            project(s)
        if KV:
            own_send(s)
            if s >= 1:
                relay(s - 1)
            if s >= 2:
                arrived(s - 2)
        if ATT and s >= 2:
            attend(0, s + 1, s - 2)
            attend_keys(s, 0, s - 2)
    for m in (msgs - 2, msgs - 1):
        if KV and m == msgs - 2:
            relay(msgs - 1)
        if KV:
            arrived(m)
        if ATT:
            attend(0, msgs, m)

    for i in range(msgs):
        for h in range(heads):
            r = i * tile + h * sub
            whole = jnp.sum(tot[r : r + sub, :], -1, keepdims=True)
            done = (acc[r : r + sub, :] / whole).astype(bf16)
            for u in (0, 1):
                there = pl.ds(pl.multiple_of(places[2 * i + u], half), half)
                out[there, h * HEAD : (h + 1) * HEAD] = done[u * half : (u + 1) * half]

    if RING:
        for k in range(7):
            ring_copy(k, True).wait_send()
            ring_copy(k, False).wait_send()
    if KV:
        for m in range(msgs):
            for cond, copy in own_copies(m) + passed_copies(m, 2) + passed_copies(m, 7):

                @pl.when(cond)
                def _(copy=copy):
                    copy.wait_send()


def tables(rows, nctx):
    freq = np.exp(-(np.arange(HEAD // 2) * (2.0 / HEAD)) * math.log(500000.0))
    fine = np.arange(rows)[:, None] * freq[None, :]
    coarse = (np.arange(nctx) * rows)[:, None] * freq[None, :]
    twice = lambda v: np.concatenate([v, v], 1).astype(np.float32)
    both = np.concatenate([twice(np.cos(coarse)), twice(np.sin(coarse))], 1)
    return twice(np.cos(fine)), twice(np.sin(fine)), both


def solution(mesh):
    nctx, nten = mesh.shape["context"], mesh.shape["tensor"]

    def body(tokens, norm_gain, w_query, key_matrix, value_matrix, seg_ids):
        sub, width = tokens.shape
        rows = sub * nten
        wide_q = w_query.shape[1]
        heads = wide_q // HEAD
        reach = 4096 // rows
        key_rows = pl.cdiv((reach + 1) * sub, HEAD) * HEAD
        ctab, stab, atab = tables(rows, nctx)

        hbm = pl.BlockSpec(memory_space=pl.ANY)
        dma = pltpu.SemaphoreType.DMA
        f32, bf16 = jnp.float32, jnp.bfloat16
        return pl.pallas_call(
            functools.partial(kernel, sub, reach, nctx, nten),
            out_shape=jax.ShapeDtypeStruct((rows, wide_q), bf16),
            in_specs=[hbm] * 9,
            out_specs=pl.BlockSpec(memory_space=pltpu.VMEM),
            scratch_shapes=[
                pltpu.VMEM((rows, width), bf16),
                pltpu.VMEM((width, wide_q + 2 * HEAD), bf16),
                pltpu.VMEM((sub, width), bf16),
                pltpu.VMEM((heads * rows, 2 * HEAD), bf16),
                pltpu.VMEM((nten, key_rows, 2 * HEAD), bf16),
                pltpu.VMEM((nten, key_rows, HEAD), bf16),
                pltpu.VMEM((rows, HEAD), f32),
                pltpu.VMEM((heads * rows, HEAD), f32),
                pltpu.VMEM((nten, 8, HEAD), f32),
                pltpu.VMEM((rows, HEAD), f32),
                pltpu.VMEM((rows, HEAD), f32),
                pltpu.VMEM((rows, HEAD), f32),
                pltpu.VMEM((rows, HEAD), f32),
                pltpu.VMEM((nctx, 2 * HEAD), f32),
                pltpu.VMEM((1, width), bf16),
                pltpu.VMEM((seg_ids.shape[0] // HEAD, HEAD), jnp.int32),
                pltpu.VMEM((heads * rows, HEAD), f32),
                pltpu.VMEM((heads * rows, HEAD), f32),
                pltpu.VMEM((heads * rows, HEAD), f32),
                dma((9,)),
                dma((7,)),
                dma((7,)),
                dma((7,)),
                dma((7,)),
                dma((4, nten)),
                dma((4, nten)),
                dma((reach + 1, nten)),
            ],
            compiler_params=pltpu.CompilerParams(
                collective_id=0, has_side_effects=True, vmem_limit_bytes=60 << 20
            ),
        )(
            tokens,
            norm_gain.reshape(1, width),
            w_query,
            key_matrix,
            value_matrix,
            seg_ids.reshape(-1, HEAD),
            ctab,
            stab,
            atab,
        )

    in_specs = (
        P(("dp", "context", "tensor"), None),
        P(),
        P(None, "tensor"),
        P(None, "tensor"),
        P(None, "tensor"),
        P("dp"),
    )
    out_specs = P(("dp", "context"), "tensor")
    return jax.shard_map(body, mesh=mesh, in_specs=in_specs, out_specs=out_specs, check_vma=False)
```

time: 96.4 us -> 75.4 us (0.78)
  Pallas kernels: 93.2 us -> 72.2 us
    pallas_call x1, Pallas kernels: 93.2 us -> 72.2 us  [body(): pl.pallas_call(functools.partial(kernel, sub, reach, nctx, nten), out_sha...]
where the time goes in v2:
time: 75.4 us; the launch traced here: 75.2 us
  Pallas kernels  72.2 us (96%)
  local copies, waits for them, and re-layouts  2.98 us (4%)
    pallas_call x1, Pallas kernels, body(): pl.pallas_call(functools.partial(kernel, sub, reach, nctx, nten), out_sha...  72.2 us
    unnamed x1, local copies, waits for them, and re-layouts  1.67 us

profile of v2, /device:TPU:6, one launch (start us, length us, event | category | flops | bytes accessed | tf_op | source)
XLA Modules:
  0.0 75.2 jit_solution(16787368318579030053)
XLA Ops:
  0.0 1.3 %reshape.6.gain = bf16[1,4096]{1,0:T(2,128)(2,1)} reshape(bf16[4096]{0:T(1024)(128)(2,1)} %param.10) | data formatting | bytes 16384 | tf_op jit(solution)/shard_map/reshape | solution.py:437
  1.3 72.2 %shard_map.91 = bf16[512,256]{1,0:T(8,128)(2,1)} custom-call(bf16[64,4096]{1,0:T(8,128)(2,1)} %tok.1, bf16[1,4096]{1,0:T(2,128)(2,1)} %reshape.6.gain, bf16[4096,256]{1,0:T(8,128)(2,1)} %wq.1, bf16[4096,128]{1,0:T(8,128)(2,1)} %wk.1, bf16[4096,128]{1,0:T(8,128)(2,1)} %wv.1, s32[64,128]{1,0:T(8,128)} %bitcast.1, f32[512,128]{1,0:T(8,128)} %constant.6.clone.ctab, ...), custom_call_target="tpu_custom_call" | custom-call | tf_op jit(solution)/shard_map/pallas_call | solution.py:398
  73.6 1.7 %copy.11 = bf16[512,256]{1,0:T(8,128)(2,1)} copy(bf16[512,256]{1,0:T(8,128)(2,1)} %shard_map.91) | data formatting | bytes 524288

commit v3 on v2

--- a/solution.py
+++ b/solution.py
@@ -21,6 +21,14 @@
 PASSED = {2: ((1, 3), (2, 4)), 7: ((-1, 6), (-2, 5))}
 EXTRA = ((6, 6), (6, 5), (5, 5))
 WAITED = (1, 3, 4, 5, 6, 8)
+PLAN = {
+    4: ((0, 4, 0, 1, 2),),
+    5: ((0, 4, 3),),
+    6: ((0, 4, 4), (4, 6, 0, 1, 2, 3, 4)),
+    7: ((6, 8, 0, 1, 2, 3, 4), (0, 4, 5), (4, 8, 5)),
+    8: ((0, 4, 6), (4, 8, 6)),
+    9: ((0, 4, 7), (4, 8, 7)),
+}
 RING = PROJ = KV = ATT = True
 
 
@@ -286,44 +294,29 @@
 
     chunks = kv.shape[1] // HEAD
 
-    def attend_rows(here, j):
-        keys = jnp.concatenate([kv[j, :, 0:HEAD], kaug[j]], 1)
-        vals = kv[j, :, HEAD : 2 * HEAD]
-        s = lax.dot_general(
-            q[here, :], keys, (((1,), (1,)), ((), ())), preferred_element_type=f32
-        )
-        cols = [s[:, i * HEAD : (i + 1) * HEAD] for i in range(chunks)]
-        cols[0] = jnp.where(kp[j][0:1, :] <= qp[here, :], cols[0], NEG)
+    def attend(lo, hi, *js):
+        here = slice(lo * tile, hi * tile)
+        queries, spots = q[here, :], qp[here, :]
+        cols = []
+        for j in js:
+            keys = jnp.concatenate([kv[j, :, 0:HEAD], kaug[j]], 1)
+            s = lax.dot_general(queries, keys, (((1,), (1,)), ((), ())), preferred_element_type=f32)
+            new = [s[:, i * HEAD : (i + 1) * HEAD] for i in range(chunks)]
+            new[0] = jnp.where(kp[j][0:1, :] <= spots, new[0], NEG)
+            cols.append(new)
         old = mx[here, :]
-        top = functools.reduce(jnp.maximum, cols)
+        top = functools.reduce(jnp.maximum, sum(cols, []))
         new = jnp.maximum(old, jnp.max(top, -1, keepdims=True))
-        p = [jnp.exp2(v - new) for v in cols]
         fade = jnp.exp2(old - new)
         mx[here, :] = new
-        tot[here, :] = tot[here, :] * fade + functools.reduce(jnp.add, p)
-        low = jnp.concatenate([v.astype(bf16) for v in p], 1)
-        acc[here, :] = acc[here, :] * fade + jnp.dot(low, vals, preferred_element_type=f32)
-
-    def attend(lo, hi, j):
-        pairs = (hi - lo) // 2
-
-        def two(i, carry):
-            r = pl.multiple_of(lo * tile + i * 2 * tile, tile)
-            attend_rows(pl.ds(r, 2 * tile), j)
-            return carry
-
-        if pairs:
-            lax.fori_loop(0, pairs, two, 0)
-        if (hi - lo) % 2:
-            attend_rows(pl.ds((hi - 1) * tile, tile), j)
-
-    def attend_keys(i, lo, hi):
-        def step(j, carry):
-            attend_rows(pl.ds(i * tile, tile), j)
-            return carry
-
-        if hi > lo:
-            lax.fori_loop(lo, hi, step, 0)
+        whole, got = tot[here, :] * fade, acc[here, :] * fade
+        for j, part in zip(js, cols):
+            p = [jnp.exp2(v - new) for v in part]
+            whole = whole + functools.reduce(jnp.add, p)
+            low = jnp.concatenate([v.astype(bf16) for v in p], 1)
+            got = got + jnp.dot(low, kv[j, :, HEAD : 2 * HEAD], preferred_element_type=f32)
+        tot[here, :] = whole
+        acc[here, :] = got
 
     for i in (0, 2, 6, 7, 8):
         loads[i].wait()
@@ -338,16 +331,17 @@
                 relay(s - 1)
             if s >= 2:
                 arrived(s - 2)
-        if ATT and s >= 2:
-            attend(0, s + 1, s - 2)
-            attend_keys(s, 0, s - 2)
+        if ATT:
+            for job in PLAN.get(s, ()):
+                attend(*job)
     for m in (msgs - 2, msgs - 1):
         if KV and m == msgs - 2:
             relay(msgs - 1)
         if KV:
             arrived(m)
         if ATT:
-            attend(0, msgs, m)
+            for job in PLAN[m + 2]:
+                attend(*job)
 
     for i in range(msgs):
         for h in range(heads):

time: 75.4 us -> 71.3 us (0.946)
  Pallas kernels: 72.2 us -> 68.2 us
    pallas_call x1, Pallas kernels: 72.2 us -> 68.2 us  [body(): pl.pallas_call(functools.partial(kernel, sub, reach, nctx, nten), out_sha...]
where the time goes in v3:
time: 71.3 us; the launch traced here: 71.2 us
  Pallas kernels  68.2 us (96%)
  local copies, waits for them, and re-layouts  2.98 us (4%)
    pallas_call x1, Pallas kernels, body(): pl.pallas_call(functools.partial(kernel, sub, reach, nctx, nten), out_sha...  68.2 us
    unnamed x1, local copies, waits for them, and re-layouts  1.67 us

profile of v3, /device:TPU:6, one launch (start us, length us, event | category | flops | bytes accessed | tf_op | source)
XLA Modules:
  0.0 71.2 jit_solution(14399043139607265071)
XLA Ops:
  0.0 1.3 %reshape.6.gain = bf16[1,4096]{1,0:T(2,128)(2,1)} reshape(bf16[4096]{0:T(1024)(128)(2,1)} %param.10) | data formatting | bytes 16384 | tf_op jit(solution)/shard_map/reshape | solution.py:431
  1.3 68.2 %shard_map.91 = bf16[512,256]{1,0:T(8,128)(2,1)} custom-call(bf16[64,4096]{1,0:T(8,128)(2,1)} %tok.1, bf16[1,4096]{1,0:T(2,128)(2,1)} %reshape.6.gain, bf16[4096,256]{1,0:T(8,128)(2,1)} %wq.1, bf16[4096,128]{1,0:T(8,128)(2,1)} %wk.1, bf16[4096,128]{1,0:T(8,128)(2,1)} %wv.1, s32[64,128]{1,0:T(8,128)} %bitcast.1, f32[512,128]{1,0:T(8,128)} %constant.6.clone.ctab, ...), custom_call_target="tpu_custom_call" | custom-call | tf_op jit(solution)/shard_map/pallas_call | solution.py:392
  69.5 1.7 %copy.11 = bf16[512,256]{1,0:T(8,128)(2,1)} copy(bf16[512,256]{1,0:T(8,128)(2,1)} %shard_map.91) | data formatting | bytes 524288

commit v4 on v3

--- a/solution.py
+++ b/solution.py
@@ -17,7 +17,7 @@
 ARRIVAL = [(0, 0), (0, 1)]
 for _k in range(7):
     ARRIVAL += [(-(1 + _k // 2), _k % 2), (1 + _k // 2, 1 - _k % 2)]
-DIRECT = (1, 2, 7, 8)
+DIRECT = (2, 7, 1, 8)
 PASSED = {2: ((1, 3), (2, 4)), 7: ((-1, 6), (-2, 5))}
 EXTRA = ((6, 6), (6, 5), (5, 5))
 WAITED = (1, 3, 4, 5, 6, 8)
@@ -150,17 +150,17 @@
             src_ref=kv.at[m, pl.ds(src_slot * sub, sub)],
             dst_ref=kv.at[m, pl.ds(dst_slot * sub, sub)],
             send_sem=sem,
-            recv_sem=kv_recv.at[dst_slot, m],
+            recv_sem=kv_recv.at[dst_slot - 1, m],
             device_id={"context": target},
             device_id_type=MESH,
         )
 
     def own_copies(m):
         res = [
-            (c + d <= last, kv_copy(m, 0, d, c + d, own_sem.at[i, m])) for i, d in enumerate(DIRECT)
+            (c + d <= last, kv_copy(m, 0, d, c + d, own_sem.at[i, m % 2])) for i, d in enumerate(DIRECT)
         ]
         for back, d in EXTRA:
-            res.append((c == last - back, kv_copy(m, 0, d, c + d, own_sem.at[d - 3, m])))
+            res.append((c == last - back, kv_copy(m, 0, d, c + d, own_sem.at[{6: 3, 5: 1}[d], m % 2])))
         return res
 
     def passed_copies(m, slot):
@@ -168,7 +168,7 @@
         return [
             (
                 (c >= slot) & (c + step <= last),
-                kv_copy(m, slot, there, c + step, fwd_sem.at[first + i, m]),
+                kv_copy(m, slot, there, c + step, fwd_sem.at[first + i, m % 2]),
             )
             for i, (step, there) in enumerate(PASSED[slot])
         ]
@@ -180,17 +180,28 @@
             def _(copy=copy):
                 copy.start()
 
+    def leave_all(copies):
+        for cond, copy in copies:
+
+            @pl.when(cond)
+            def _(copy=copy):
+                copy.wait_send()
+
     def landed(m, d):
         @pl.when(c >= d)
         def _():
-            kv_copy(m, d, d, c, own_sem.at[0, m]).wait_recv()
+            kv_copy(m, d, d, c, own_sem.at[0, m % 2]).wait_recv()
 
     def own_send(m):
+        if m >= 2:
+            leave_all(own_copies(m - 2))
         start_all(own_copies(m))
 
     def relay(m):
         for slot in PASSED:
             landed(m, slot)
+            if m >= 2:
+                leave_all(passed_copies(m - 2, slot))
             start_all(passed_copies(m, slot))
 
     def arrived(m):
@@ -268,7 +279,11 @@
 
     scale = math.log2(math.e) / math.sqrt(HEAD)
 
-    def project(m):
+    def rotate(v, r0):
+        here = slice(r0, r0 + sub)
+        return v * cosv[here, :] + pltpu.roll(v, HEAD // 2, 1) * sinv[here, :]
+
+    def project_keys(m):
         r0 = m * sub
 
         def norm(i, carry):
@@ -280,17 +295,16 @@
             return carry
 
         lax.fori_loop(0, sub // 16, norm, 0)
-        got = jnp.dot(nrm[...], w[...], preferred_element_type=f32)
-        cs, sn = cosv[r0 : r0 + sub, :], sinv[r0 : r0 + sub, :]
-
-        def rotate(v):
-            return v * cs + pltpu.roll(v, HEAD // 2, 1) * sn
-
-        kv[m, 0:sub, 0:HEAD] = rotate(got[:, wide_q : wide_q + HEAD]).astype(bf16)
-        kv[m, 0:sub, HEAD : 2 * HEAD] = got[:, wide_q + HEAD :].astype(bf16)
+        got = jnp.dot(nrm[...], w[:, wide_q:], preferred_element_type=f32)
+        kv[m, 0:sub, 0:HEAD] = rotate(got[:, 0:HEAD], r0).astype(bf16)
+        kv[m, 0:sub, HEAD : 2 * HEAD] = got[:, HEAD:].astype(bf16)
+
+    def project_queries(m):
+        got = jnp.dot(nrm[...], w[:, 0:wide_q], preferred_element_type=f32)
         for h in range(heads):
             r = m * tile + h * sub
-            q[r : r + sub, 0:HEAD] = (rotate(got[:, h * HEAD : (h + 1) * HEAD]) * scale).astype(bf16)
+            v = rotate(got[:, h * HEAD : (h + 1) * HEAD], m * sub)
+            q[r : r + sub, 0:HEAD] = (v * scale).astype(bf16)
 
     chunks = kv.shape[1] // HEAD
 
@@ -324,13 +338,15 @@
         if RING and s >= 1:
             ring_step(s - 1)
         if PROJ:
-            project(s)
+            project_keys(s)
         if KV:
             own_send(s)
             if s >= 1:
                 relay(s - 1)
-            if s >= 2:
-                arrived(s - 2)
+        if PROJ:
+            project_queries(s)
+        if KV and s >= 2:
+            arrived(s - 2)
         if ATT:
             for job in PLAN.get(s, ()):
                 attend(*job)
@@ -357,12 +373,8 @@
             ring_copy(k, True).wait_send()
             ring_copy(k, False).wait_send()
     if KV:
-        for m in range(msgs):
-            for cond, copy in own_copies(m) + passed_copies(m, 2) + passed_copies(m, 7):
-
-                @pl.when(cond)
-                def _(copy=copy):
-                    copy.wait_send()
+        for m in (msgs - 2, msgs - 1):
+            leave_all(own_copies(m) + passed_copies(m, 2) + passed_copies(m, 7))
 
 
 def tables(rows, nctx):
@@ -419,9 +431,9 @@
                 dma((7,)),
                 dma((7,)),
                 dma((7,)),
-                dma((4, nten)),
-                dma((4, nten)),
-                dma((reach + 1, nten)),
+                dma((4, 2)),
+                dma((4, 2)),
+                dma((reach, nten)),
             ],
             compiler_params=pltpu.CompilerParams(
                 collective_id=0, has_side_effects=True, vmem_limit_bytes=60 << 20

time: 71.3 us -> 70.6 us (level)
  no operation moved by 1% of the time
where the time goes in v4:
time: 70.6 us; the launch traced here: 70.5 us
  Pallas kernels  67.5 us (96%)
  local copies, waits for them, and re-layouts  2.98 us (4%)
    pallas_call x1, Pallas kernels, body(): pl.pallas_call(functools.partial(kernel, sub, reach, nctx, nten), out_sha...  67.5 us
    unnamed x1, local copies, waits for them, and re-layouts  1.67 us

profile of v4, /device:TPU:6, one launch (start us, length us, event | category | flops | bytes accessed | tf_op | source)
XLA Modules:
  0.0 70.5 jit_solution(231672824840490641)
XLA Ops:
  0.0 1.3 %reshape.6.gain = bf16[1,4096]{1,0:T(2,128)(2,1)} reshape(bf16[4096]{0:T(1024)(128)(2,1)} %param.10) | data formatting | bytes 16384 | tf_op jit(solution)/shard_map/reshape | solution.py:443
  1.3 67.5 %shard_map.91 = bf16[512,256]{1,0:T(8,128)(2,1)} custom-call(bf16[64,4096]{1,0:T(8,128)(2,1)} %tok.1, bf16[1,4096]{1,0:T(2,128)(2,1)} %reshape.6.gain, bf16[4096,256]{1,0:T(8,128)(2,1)} %wq.1, bf16[4096,128]{1,0:T(8,128)(2,1)} %wk.1, bf16[4096,128]{1,0:T(8,128)(2,1)} %wv.1, s32[64,128]{1,0:T(8,128)} %bitcast.1, f32[512,128]{1,0:T(8,128)} %constant.6.clone.ctab, ...), custom_call_target="tpu_custom_call" | custom-call | tf_op jit(solution)/shard_map/pallas_call | solution.py:404
  68.8 1.7 %copy.11 = bf16[512,256]{1,0:T(8,128)(2,1)} copy(bf16[512,256]{1,0:T(8,128)(2,1)} %shard_map.91) | data formatting | bytes 524288
